TPU v7x, 256 devices: a whole 4x4x8 slice. The times are simulated.
256 devices in a mesh: tile: 32 (over x, y, core), mode: 8 (over z).
Axes of the slice: x: 4, y: 4, z: 8, core: 2. Of those that a mesh axis runs over, the one named last changes fastest.
Arguments:
- mode_shapes: bfloat16 [64, 256, 2048], P('mode', 'tile'), may hold values from -6 to 6
- stiffness: float32 [256, 2048], P('tile'), may hold values from 0.5 to 4
- node_slot: int32 [256, 2048], P('tile'), may hold values from 0 to 255, as said below
- slot_zone: int32 [32, 32, 8], replicated, may hold values from 0 to 15, as said below
Outputs:
- energy: float32 [512, 64, 64], P('tile', 'mode')
Inputs may be any that keep to these rules, and one draw needn't show every extreme that they name: `slot_zone`: for each tile and owner, the 8 zone numbers are distinct. `node_slot`: slots that no node of a tile names carry no zone's nodes.
All inputs are finite; a program needn't handle non-finite values.
Results may differ from a plain program's by a relative error of at most 0.00099.
Values may be sent and summed in bfloat16 or wider, within the bound.
No kernel may reach another device: no remote copies, remote signals or barrier semaphores. Data moves between devices by JAX's collectives and lax.ppermute only.
A program may use at most 64 MiB of HBM per device.

v0:
```python
import math
import jax
import jax.numpy as jnp
from jax import lax
from jax.sharding import PartitionSpec as P

ZONES = 512
POISSON = 0.3
SHEAR = 2.0 * (1.0 - POISSON)


def with_halo(cells, sides, width):
    for axis, dim in sides:
        count = lax.axis_size(axis)
        ends = count - 1
        head = lax.slice_in_dim(cells, 0, width, axis=dim)
        tail = lax.slice_in_dim(cells, cells.shape[dim] - width, cells.shape[dim], axis=dim)
        cells = jnp.concatenate(
            [
                lax.ppermute(tail, axis, [(i, (i + 1) % count) for i in range(ends)]),
                cells,
                lax.ppermute(head, axis, [((i + 1) % count, i) for i in range(ends)]),
            ],
            axis=dim,
        )
    return cells


def curvatures(shapes_framed):
    framed = jnp.pad(shapes_framed, ((0, 0), (0, 0), (1, 1)))
    centre = framed[:, 1:-1, 1:-1]
    along_x = framed[:, 2:, 1:-1] - 2.0 * centre + framed[:, :-2, 1:-1]
    along_y = framed[:, 1:-1, 2:] - 2.0 * centre + framed[:, 1:-1, :-2]
    twist_xy = 0.25 * (
        framed[:, 2:, 2:] - framed[:, 2:, :-2] - framed[:, :-2, 2:] + framed[:, :-2, :-2]
    )
    return jnp.stack([along_x, along_y, twist_xy]).astype(jnp.bfloat16)


def left_factor(bending, stiffness):
    along_x, along_y, twist_xy = (bending[0], bending[1], bending[2])
    return jnp.stack(
        [
            stiffness * (along_x + POISSON * along_y),
            stiffness * (along_y + POISSON * along_x),
            stiffness * (SHEAR * twist_xy),
        ]
    )


def per_device(mode_shapes, stiffness, node_slot, slot_zone):
    panel_modes, tile_rows, row_cells = mode_shapes.shape
    node_count = tile_rows * row_cells
    tile_count = lax.axis_size("tile")
    mode_count = panel_modes * lax.axis_size("mode")
    owner_slots = slot_zone.shape[2]
    slot_count = tile_count * owner_slots
    owned_zones = ZONES // tile_count
    pair_count = panel_modes * mode_count
    padded = with_halo(mode_shapes, (("tile", 1),), 1)
    own_bending = curvatures(padded.astype(jnp.float32))
    own_float = own_bending.astype(jnp.float32)
    weighted = left_factor(own_float, stiffness)
    own_sums = jnp.sum(weighted * own_float, axis=(0, 2, 3))
    placed_sums = lax.dynamic_update_slice_in_dim(
        jnp.zeros((mode_count,), jnp.float32), own_sums, lax.axis_index("mode") * panel_modes, 0
    )
    totals = 0.5 * lax.psum(placed_sums, ("tile", "mode"))
    gathered_bend = lax.all_gather(own_bending, "mode", axis=1, tiled=True)
    right_flat = gathered_bend.reshape(3, mode_count, node_count)
    left_flat = weighted.astype(jnp.bfloat16).reshape(3, panel_modes, node_count)
    slot_flat = node_slot.reshape(node_count)
    slot_range = jnp.arange(slot_count, dtype=jnp.int32)
    block_nodes = math.gcd(node_count, max(128, (1 << 20) // pair_count))

    def one_block(number, running):
        first_node = number * block_nodes
        left_block = lax.dynamic_slice_in_dim(left_flat, first_node, block_nodes, 2).astype(
            jnp.float32
        )
        right_block = lax.dynamic_slice_in_dim(right_flat, first_node, block_nodes, 2).astype(
            jnp.float32
        )
        slot_block = lax.dynamic_slice_in_dim(slot_flat, first_node, block_nodes, 0)
        products = jnp.sum(left_block[:, :, None, :] * right_block[:, None, :, :], axis=0)
        products = products.reshape(pair_count, block_nodes)
        member_block = (slot_block[:, None] == slot_range[None, :]).astype(jnp.float32)
        return running + jnp.dot(products, member_block, precision=lax.Precision.HIGHEST)

    by_pair = lax.fori_loop(
        0, node_count // block_nodes, one_block, jnp.zeros((pair_count, slot_count), jnp.float32)
    )
    routed = by_pair.T.reshape(tile_count, owner_slots, pair_count)
    tile_index = lax.axis_index("tile")
    own_lists = lax.dynamic_index_in_dim(slot_zone, tile_index, 0, keepdims=False)
    selector = (
        own_lists[:, :, None] == jnp.arange(owned_zones, dtype=jnp.int32)[None, None, :]
    ).astype(jnp.float32)
    spread_zones = jnp.einsum("dcz,dcm->dzm", selector, routed, precision=lax.Precision.HIGHEST)
    spread_zones = spread_zones.reshape(tile_count * owned_zones, pair_count)
    summed = lax.psum_scatter(spread_zones, "tile", scatter_dimension=0, tiled=True)
    own_totals = lax.dynamic_slice_in_dim(
        totals, lax.axis_index("mode") * panel_modes, panel_modes, 0
    )
    denominator = jnp.sqrt(own_totals[:, None] * totals[None, :])
    return ZONES * (0.5 * summed.reshape(owned_zones, panel_modes, mode_count)) / denominator


def solution(mesh):
    placed = (P("mode", "tile", None), P("tile", None), P("tile", None), P())
    return jax.shard_map(
        per_device, mesh=mesh, in_specs=placed, out_specs=P("tile", "mode", None), check_vma=False
    )
```

profile of v0, /device:TPU:4, one launch (start us, length us, event | category | flops | bytes accessed | tf_op | source)
XLA Modules:
  0.0 281.9 jit_solution(18030605691731812583)
XLA Ops:
  6.5 1.2 fusion.25
  7.7 1.9 collective-permute-start
  9.6 5.8 %collective-permute-start.1 = (bf16[8,1,2048]{2,1,0:T(2,128)(2,1)S(1)}, bf16[8,1,2048]{2,1,0:T(2,128)(2,1)S(1)}, u32[]{:S(2)}, u32[]{:S(2)}) collective-permute-start(bf16[8,1,2048]{2,1,0:T(2,128)(2,1)S(1)} %get-tuple-element.161), channel_id=1, source_target_pairs={{8,0},{16,8},{24,16},{32,24},{40,32},{48,40},{56,48},{64,56},{72,6... | collective-permute-start | bytes 98312 | tf_op jit(solution)/shard_map/ppermute | solution.py:22
  15.4 1.9 collective-permute-done.1
  17.3 1.2 maximum_convert_fusion
  18.5 0.9 fusion.17
  19.4 1.0 pad_maximum_fusion
  21.3 2.2 fusion.22
  23.5 1.1 stack.34
  24.6 1.1 stack.35
  25.6 1.1 stack.36
  26.8 71.7 %all-gather.2.cloned.1.call-done = bf16[3,64,8,2048]{3,2,1,0:T(8,128)(2,1)} async-done(((bf16[3,8,8,2048]{3,2,1,0:T(8,128)(2,1)}), bf16[3,64,8,2048]{3,2,1,0:T(8,128)(2,1)}) %all-gather.2.cloned.1.call-update) | async-done | bytes 6291472 | tf_op jit(solution)/shard_map/all_gather | solution.py:69
  98.5 10.4 %reshape.64 = bf16[3,64,16384]{2,1,0:T(8,128)(2,1)} reshape(bf16[3,64,8,2048]{3,2,1,0:T(8,128)(2,1)} %all-gather.2.cloned.1.call-done) | data formatting | bytes 12582912 | tf_op jit(solution)/shard_map/reshape | solution.py:70
  108.9 78.5 %while.14 = (s32[]{:T(128)}, f32[512,256]{1,0:T(8,128)S(1)}, bf16[3,8,16384]{2,1,0:T(8,128)(2,1)S(1)}, bf16[3,64,16384]{2,1,0:T(8,128)(2,1)}, s32[16384]{0:T(102...) while((s32[]{:T(128)}, f32[512,256]{1,0:T(8,128)S(1)}, bf16[3,8,16384]{2,1,0:T(8,128)(2,1)S(1)}, ...), condition=%wide.region_2.3_spmd.clone, body=%wide.region_0.0_spmd.clone.sunk | while | flops 3227697152 | bytes 13885601 | solution.py:90
  108.9 1.3 dynamic-slice_convert_fusion.4
  110.2 3.1 %multiply_reduce_fusion.2 = f32[8,64,2048]{2,1,0:T(8,128)} fusion(f32[3,64,2048]{2,1,0:T(8,128)S(1)} %dynamic-slice_convert_fusion.4, f32[3,8,2048]{2,1,0:T(8,128)S(1)} %dynamic-slice_convert_fusion.5), kind=kLoop, calls=%fused_computation.1.clone.1 | loop fusion | flops 5242880 | bytes 5963776 | tf_op jit(solution)/shard_map/while/body/eval_jaxpr/reduce_sum | solution.py:85
  113.3 0.7 dynamic_slice.41
  114.0 4.7 %fusion.30 = f32[512,256]{1,0:T(8,128)S(1)} fusion(f32[512,2048]{1,0:T(8,128)} %bitcast.30, s32[2048]{0:T(1024)S(1)} %dynamic_slice.41, f32[512,256]{1,0:T(8,128)S(1)} %get-tuple-element.203, pred[]{:T(512)S(6)} %compare.4), kind=kOutput, calls=%fused_computation.4.clone.1 | convolution fusion | flops 3222011904 | bytes 5251073 | tf_op jit(solution)/shard_map/while/body/eval_jaxpr/dot_general | solution.py:88
  118.7 1.3 dynamic-slice_convert_fusion.4
  120.0 3.1 %multiply_reduce_fusion.2 = f32[8,64,2048]{2,1,0:T(8,128)} fusion(f32[3,64,2048]{2,1,0:T(8,128)S(1)} %dynamic-slice_convert_fusion.4, f32[3,8,2048]{2,1,0:T(8,128)S(1)} %dynamic-slice_convert_fusion.5), kind=kLoop, calls=%fused_computation.1.clone.1 | loop fusion | flops 5242880 | bytes 5963776 | tf_op jit(solution)/shard_map/while/body/eval_jaxpr/reduce_sum | solution.py:85
  123.1 0.7 dynamic_slice.41
  123.8 4.7 %fusion.30 = f32[512,256]{1,0:T(8,128)S(1)} fusion(f32[512,2048]{1,0:T(8,128)} %bitcast.30, s32[2048]{0:T(1024)S(1)} %dynamic_slice.41, f32[512,256]{1,0:T(8,128)S(1)} %get-tuple-element.203, pred[]{:T(512)S(6)} %compare.4), kind=kOutput, calls=%fused_computation.4.clone.1 | convolution fusion | flops 3222011904 | bytes 5251073 | tf_op jit(solution)/shard_map/while/body/eval_jaxpr/dot_general | solution.py:88
  128.5 1.3 dynamic-slice_convert_fusion.4
  129.9 3.1 %multiply_reduce_fusion.2 = f32[8,64,2048]{2,1,0:T(8,128)} fusion(f32[3,64,2048]{2,1,0:T(8,128)S(1)} %dynamic-slice_convert_fusion.4, f32[3,8,2048]{2,1,0:T(8,128)S(1)} %dynamic-slice_convert_fusion.5), kind=kLoop, calls=%fused_computation.1.clone.1 | loop fusion | flops 5242880 | bytes 5963776 | tf_op jit(solution)/shard_map/while/body/eval_jaxpr/reduce_sum | solution.py:85
  132.9 0.7 dynamic_slice.41
  133.6 4.7 %fusion.30 = f32[512,256]{1,0:T(8,128)S(1)} fusion(f32[512,2048]{1,0:T(8,128)} %bitcast.30, s32[2048]{0:T(1024)S(1)} %dynamic_slice.41, f32[512,256]{1,0:T(8,128)S(1)} %get-tuple-element.203, pred[]{:T(512)S(6)} %compare.4), kind=kOutput, calls=%fused_computation.4.clone.1 | convolution fusion | flops 3222011904 | bytes 5251073 | tf_op jit(solution)/shard_map/while/body/eval_jaxpr/dot_general | solution.py:88
  138.3 1.3 dynamic-slice_convert_fusion.4
  139.7 3.1 %multiply_reduce_fusion.2 = f32[8,64,2048]{2,1,0:T(8,128)} fusion(f32[3,64,2048]{2,1,0:T(8,128)S(1)} %dynamic-slice_convert_fusion.4, f32[3,8,2048]{2,1,0:T(8,128)S(1)} %dynamic-slice_convert_fusion.5), kind=kLoop, calls=%fused_computation.1.clone.1 | loop fusion | flops 5242880 | bytes 5963776 | tf_op jit(solution)/shard_map/while/body/eval_jaxpr/reduce_sum | solution.py:85
  142.7 0.7 dynamic_slice.41
  143.4 4.7 %fusion.30 = f32[512,256]{1,0:T(8,128)S(1)} fusion(f32[512,2048]{1,0:T(8,128)} %bitcast.30, s32[2048]{0:T(1024)S(1)} %dynamic_slice.41, f32[512,256]{1,0:T(8,128)S(1)} %get-tuple-element.203, pred[]{:T(512)S(6)} %compare.4), kind=kOutput, calls=%fused_computation.4.clone.1 | convolution fusion | flops 3222011904 | bytes 5251073 | tf_op jit(solution)/shard_map/while/body/eval_jaxpr/dot_general | solution.py:88
  148.1 1.3 dynamic-slice_convert_fusion.4
  149.5 3.1 %multiply_reduce_fusion.2 = f32[8,64,2048]{2,1,0:T(8,128)} fusion(f32[3,64,2048]{2,1,0:T(8,128)S(1)} %dynamic-slice_convert_fusion.4, f32[3,8,2048]{2,1,0:T(8,128)S(1)} %dynamic-slice_convert_fusion.5), kind=kLoop, calls=%fused_computation.1.clone.1 | loop fusion | flops 5242880 | bytes 5963776 | tf_op jit(solution)/shard_map/while/body/eval_jaxpr/reduce_sum | solution.py:85
  152.6 0.7 dynamic_slice.41
  153.3 4.7 %fusion.30 = f32[512,256]{1,0:T(8,128)S(1)} fusion(f32[512,2048]{1,0:T(8,128)} %bitcast.30, s32[2048]{0:T(1024)S(1)} %dynamic_slice.41, f32[512,256]{1,0:T(8,128)S(1)} %get-tuple-element.203, pred[]{:T(512)S(6)} %compare.4), kind=kOutput, calls=%fused_computation.4.clone.1 | convolution fusion | flops 3222011904 | bytes 5251073 | tf_op jit(solution)/shard_map/while/body/eval_jaxpr/dot_general | solution.py:88
  158.0 1.3 dynamic-slice_convert_fusion.4
  159.3 3.1 %multiply_reduce_fusion.2 = f32[8,64,2048]{2,1,0:T(8,128)} fusion(f32[3,64,2048]{2,1,0:T(8,128)S(1)} %dynamic-slice_convert_fusion.4, f32[3,8,2048]{2,1,0:T(8,128)S(1)} %dynamic-slice_convert_fusion.5), kind=kLoop, calls=%fused_computation.1.clone.1 | loop fusion | flops 5242880 | bytes 5963776 | tf_op jit(solution)/shard_map/while/body/eval_jaxpr/reduce_sum | solution.py:85
  163.1 4.7 %fusion.30 = f32[512,256]{1,0:T(8,128)S(1)} fusion(f32[512,2048]{1,0:T(8,128)} %bitcast.30, s32[2048]{0:T(1024)S(1)} %dynamic_slice.41, f32[512,256]{1,0:T(8,128)S(1)} %get-tuple-element.203, pred[]{:T(512)S(6)} %compare.4), kind=kOutput, calls=%fused_computation.4.clone.1 | convolution fusion | flops 3222011904 | bytes 5251073 | tf_op jit(solution)/shard_map/while/body/eval_jaxpr/dot_general | solution.py:88
  167.8 1.3 dynamic-slice_convert_fusion.4
  169.1 3.1 %multiply_reduce_fusion.2 = f32[8,64,2048]{2,1,0:T(8,128)} fusion(f32[3,64,2048]{2,1,0:T(8,128)S(1)} %dynamic-slice_convert_fusion.4, f32[3,8,2048]{2,1,0:T(8,128)S(1)} %dynamic-slice_convert_fusion.5), kind=kLoop, calls=%fused_computation.1.clone.1 | loop fusion | flops 5242880 | bytes 5963776 | tf_op jit(solution)/shard_map/while/body/eval_jaxpr/reduce_sum | solution.py:85
  172.9 4.7 %fusion.30 = f32[512,256]{1,0:T(8,128)S(1)} fusion(f32[512,2048]{1,0:T(8,128)} %bitcast.30, s32[2048]{0:T(1024)S(1)} %dynamic_slice.41, f32[512,256]{1,0:T(8,128)S(1)} %get-tuple-element.203, pred[]{:T(512)S(6)} %compare.4), kind=kOutput, calls=%fused_computation.4.clone.1 | convolution fusion | flops 3222011904 | bytes 5251073 | tf_op jit(solution)/shard_map/while/body/eval_jaxpr/dot_general | solution.py:88
  177.6 1.3 dynamic-slice_convert_fusion.4
  178.9 3.1 %multiply_reduce_fusion.2 = f32[8,64,2048]{2,1,0:T(8,128)} fusion(f32[3,64,2048]{2,1,0:T(8,128)S(1)} %dynamic-slice_convert_fusion.4, f32[3,8,2048]{2,1,0:T(8,128)S(1)} %dynamic-slice_convert_fusion.5), kind=kLoop, calls=%fused_computation.1.clone.1 | loop fusion | flops 5242880 | bytes 5963776 | tf_op jit(solution)/shard_map/while/body/eval_jaxpr/reduce_sum | solution.py:85
  182.0 0.7 dynamic_slice.41
  182.7 4.7 %fusion.30 = f32[512,256]{1,0:T(8,128)S(1)} fusion(f32[512,2048]{1,0:T(8,128)} %bitcast.30, s32[2048]{0:T(1024)S(1)} %dynamic_slice.41, f32[512,256]{1,0:T(8,128)S(1)} %get-tuple-element.203, pred[]{:T(512)S(6)} %compare.4), kind=kOutput, calls=%fused_computation.4.clone.1 | convolution fusion | flops 3222011904 | bytes 5251073 | tf_op jit(solution)/shard_map/while/body/eval_jaxpr/dot_general | solution.py:88
  187.6 1.9 fusion.15
  190.1 74.7 %psum.7 = f32[64]{0:T(128)S(1)} all-reduce(f32[64]{0:T(128)S(1)} %dynamic_update_slice.3), channel_id=1, replica_groups=mesh['tile'=32,'mode'=8] {'tile','mode'}, use_global_device_ids=true, to_apply=%region_5.6 | all-reduce | flops 64 | bytes 512 | tf_op jit(solution)/shard_map/psum | solution.py:68
  264.9 8.6 %reduce-scatter.2.cloned.1.call-done = f32[16,512]{1,0:T(8,128)} async-done(((f32[512,512]{1,0:T(8,128)}), f32[16,512]{1,0:T(8,128)}) %reduce-scatter.2.cloned.1.call-update) | async-done | bytes 32784 | tf_op jit(solution)/shard_map/reduce_scatter | solution.py:101
  273.5 0.8 broadcast_multiply_fusion.1
  (40 shorter events, 4.1 us)
Async XLA Ops:
  6.5 14.6 %copy-start = (s32[32,32,8]{1,2,0:T(8,128)S(1)}, s32[32,32,8]{1,2,0:T(8,128)}, u32[]{:S(2)}) copy-start(s32[32,32,8]{1,2,0:T(8,128)} %param.9) | copy-start | bytes 98308
  6.5 91.9 %all-gather.2.cloned.1.call-start = ((), (), s32[]{:S(2)}) async-start(), calls=%async_computation.1 | async-start | bytes 7077888 | tf_op jit(solution)/shard_map/all_gather | solution.py:69
  7.7 7.7 %collective-permute-start = (bf16[8,1,2048]{2,1,0:T(2,128)(2,1)S(1)}, bf16[8,1,2048]{2,1,0:T(2,128)(2,1)S(1)}, u32[]{:S(2)}, u32[]{:S(2)}) collective-permute-start(bf16[8,1,2048]{2,1,0:T(2,128)(2,1)S(1)} %get-tuple-element.160), channel_id=1, source_target_pairs={{0,8},{8,16},{16,24},{24,32},{32,40},{40,48},{48,56},{56,64},{64,7... | collective-permute-start | bytes 98312 | tf_op jit(solution)/shard_map/ppermute | solution.py:20
  9.6 7.6 %collective-permute-start.1 = (bf16[8,1,2048]{2,1,0:T(2,128)(2,1)S(1)}, bf16[8,1,2048]{2,1,0:T(2,128)(2,1)S(1)}, u32[]{:S(2)}, u32[]{:S(2)}) collective-permute-start(bf16[8,1,2048]{2,1,0:T(2,128)(2,1)S(1)} %get-tuple-element.161), channel_id=1, source_target_pairs={{8,0},{16,8},{24,16},{32,24},{40,32},{48,40},{56,48},{64,56},{72,6... | collective-permute-start | bytes 98312 | tf_op jit(solution)/shard_map/ppermute | solution.py:22
  19.4 1.2 copy-start.4
  19.4 1.9 copy-start.3
  20.5 253.1 %reduce-scatter.2.cloned.1.call-start = ((), (), s32[]{:S(2)}) async-start(), calls=%async_computation.2 | async-start | bytes 1081344 | tf_op jit(solution)/shard_map/reduce_scatter | solution.py:101
  187.6 2.0 copy-start.1
  187.6 2.0 copy-start.2
Sparse Core Ops, SparseCore 0:
  20.6 77.8 all-gather.1
  189.7 83.7 reduce-scatter.1
where the time goes:
time: 283 us; the launch traced here: 282 us
  waiting for transfers between devices  82.2 us (29%)
  blocking collectives  74.7 us (26%)
  other arithmetic  42.3 us (15%)
  matrix products  39.4 us (14%)
  local copies, waits for them, and re-layouts  21.7 us (8%)
  between operations  13.5 us (5%)
  starting transfers between devices  7.72 us (3%)
    psum x1, blocking collectives, per_device(): totals = 0.5 * lax.psum(placed_sums, ('tile', 'mode'))  74.7 us
    all_gather x1, waiting for transfers between devices, per_device(): gathered_bend = lax.all_gather(own_bending, 'mode', axis=1, tiled=True)  71.7 us
    dot_general x8, matrix products, one_block(): jnp.dot(products, member_block, precision=lax.Precision.HIGHEST)  37.5 us
    reduce_sum x8, other arithmetic, one_block(): jnp.sum(left_block[:, :, None, :] * right_block[:, None, :, :], axis=0)  24.5 us
    reshape x1, local copies, waits for them, and re-layouts, per_device(): right_flat = gathered_bend.reshape(3, mode_count, node_count)  10.4 us
    convert_element_type x8, other arithmetic, one_block(): lax.dynamic_slice_in_dim(right_flat, first_node, block_nodes, 2)  10.4 us
    reduce_scatter x1, waiting for transfers between devices, per_device(): lax.psum_scatter(spread_zones, 'tile', scatter_dimension=0, tiled=True)  8.6 us
    ppermute x1, starting transfers between devices, with_halo(): lax.ppermute(head, axis, [((i + 1) % count, i) for i in range(ends)])  5.75 us
  transfers between devices with their start and end apart: 4, of which 3 were waited for; matrix products, arithmetic and copies ran while one was open for 2% of the time, Pallas kernels for 0%

commit v1 on v0

--- a/solution.py
+++ b/solution.py
@@ -66,7 +66,9 @@
         jnp.zeros((mode_count,), jnp.float32), own_sums, lax.axis_index("mode") * panel_modes, 0
     )
     totals = 0.5 * lax.psum(placed_sums, ("tile", "mode"))
-    gathered_bend = lax.all_gather(own_bending, "mode", axis=1, tiled=True)
+    gathered_bend = jnp.concatenate(
+        lax.all_to_all(jnp.stack([own_bending] * lax.axis_size("mode")), "mode", 0, 0), axis=1
+    )
     right_flat = gathered_bend.reshape(3, mode_count, node_count)
     left_flat = weighted.astype(jnp.bfloat16).reshape(3, panel_modes, node_count)
     slot_flat = node_slot.reshape(node_count)

time: 283 us -> 366 us (1.29)
  waiting for transfers between devices: 82.2 us -> 145 us
  local copies, waits for them, and re-layouts: 21.7 us -> 36 us
  starting transfers between devices: 7.72 us -> 16.5 us
    all_to_all x0 -> x1, waiting for transfers between devices: none -> 135 us  [per_device(): lax.all_to_all(jnp.stack([own_bending] * lax.axis_size('mode')), 'mode',...]
    all_gather x1 -> x0, waiting for transfers between devices: 71.7 us -> none  [per_device(): gathered_bend = lax.all_gather(own_bending, 'mode', axis=1, tiled=True)]
    another operation x0 -> x3, local copies, waits for them, and re-layouts: none -> 14.3 us  [the longest x1 10.4 us: per_device(): right_flat = gathered_bend.reshape(3, mode_count, node_count)]
    all_to_all x0 -> x1, starting transfers between devices: none -> 8.6 us  [per_device(): lax.all_to_all(jnp.stack([own_bending] * lax.axis_size('mode')), 'mode',...]
where the time goes in v1:
time: 366 us; the launch traced here: 364 us
  waiting for transfers between devices  145 us (40%)
  blocking collectives  72.6 us (20%)
  other arithmetic  41.5 us (11%)
  matrix products  39.4 us (11%)
  local copies, waits for them, and re-layouts  36 us (10%)
  starting transfers between devices  16.5 us (5%)
  between operations  13.5 us (4%)
    all_to_all x1, waiting for transfers between devices, per_device(): lax.all_to_all(jnp.stack([own_bending] * lax.axis_size('mode')), 'mode',...  135 us
    psum x1, blocking collectives, per_device(): totals = 0.5 * lax.psum(placed_sums, ('tile', 'mode'))  72.6 us
    dot_general x8, matrix products, one_block(): jnp.dot(products, member_block, precision=lax.Precision.HIGHEST)  37.5 us
    reduce_sum x8, other arithmetic, one_block(): jnp.sum(left_block[:, :, None, :] * right_block[:, None, :, :], axis=0)  24.6 us
    reshape x1, local copies, waits for them, and re-layouts, per_device(): jnp.concatenate(lax.all_to_all(jnp.stack([own_bending] * lax.axis_size('m...  10.4 us
    another operation x1, local copies, waits for them, and re-layouts, per_device(): right_flat = gathered_bend.reshape(3, mode_count, node_count)  10.4 us
    convert_element_type x8, other arithmetic, one_block(): lax.dynamic_slice_in_dim(right_flat, first_node, block_nodes, 2)  10.4 us
    all_to_all x1, starting transfers between devices, per_device(): lax.all_to_all(jnp.stack([own_bending] * lax.axis_size('mode')), 'mode',...  8.6 us
  transfers between devices with their start and end apart: 4, of which 3 were waited for; matrix products, arithmetic and copies ran while one was open for 2% of the time, Pallas kernels for 0%

profile of v1, /device:TPU:4, one launch (start us, length us, event | category | flops | bytes accessed | tf_op | source)
XLA Modules:
  0.0 364.4 jit_solution(7498594519757578848)
XLA Ops:
  6.5 1.2 fusion.25
  7.7 1.9 collective-permute-start
  9.6 5.8 %collective-permute-start.1 = (bf16[8,1,2048]{2,1,0:T(2,128)(2,1)S(1)}, bf16[8,1,2048]{2,1,0:T(2,128)(2,1)S(1)}, u32[]{:S(2)}, u32[]{:S(2)}) collective-permute-start(bf16[8,1,2048]{2,1,0:T(2,128)(2,1)S(1)} %get-tuple-element.161), channel_id=1, source_target_pairs={{8,0},{16,8},{24,16},{32,24},{40,32},{48,40},{56,48},{64,56},{72,6... | collective-permute-start | bytes 98312 | tf_op jit(solution)/shard_map/ppermute | solution.py:22
  15.4 1.9 collective-permute-done.1
  17.3 1.2 maximum_convert_fusion
  18.5 0.9 fusion.17
  20.0 3.5 stack.49
  23.4 8.6 %all-to-all-start = ((bf16[8,3,8,8,2048]{4,2,3,1,0:T(8,128)(2,1)}), bf16[8,3,8,8,2048]{4,2,3,1,0:T(8,128)(2,1)}, u32[]{:S(2)}, u32[]{:S(2)}) async-start(bf16[8,3,8,8,2048]{4,2,3,1,0:T(8,128)(2,1)} %stack.49), calls=%async_computation | async-start | bytes 12582912 | tf_op jit(solution)/shard_map/all_to_all | solution.py:70
  33.0 2.2 fusion.22
  35.2 1.1 stack.45
  36.3 1.1 stack.46
  37.4 1.1 stack.47
  38.6 134.8 %all-to-all-done = bf16[8,3,8,8,2048]{4,2,3,1,0:T(8,128)(2,1)} async-done(((bf16[8,3,8,8,2048]{4,2,3,1,0:T(8,128)(2,1)}), bf16[8,3,8,8,2048]{4,2,3,1,0:T(8,128)(2,1)}, u32[]{:S(2)}, u32[]{:S(2)}) %all-to-all-start) | async-done | bytes 6291488 | tf_op jit(solution)/shard_map/all_to_all | solution.py:70
  173.4 10.4 %copy.19 = bf16[3,8,8,8,2048]{4,3,2,1,0:T(8,128)(2,1)} copy(bf16[3,8,8,8,2048]{4,2,3,0,1:T(8,128)(2,1)} %bitcast.4) | data formatting | bytes 12582912 | tf_op jit(solution)/shard_map/reshape | solution.py:69
  183.8 10.4 %reshape_reshape.3 = bf16[3,64,16384]{2,1,0:T(8,128)(2,1)} reshape(bf16[3,8,8,8,2048]{4,3,2,1,0:T(8,128)(2,1)} %copy.19) | data formatting | bytes 12582912 | tf_op jit(solution)/shard_map/reshape;reshape | solution.py:72
  194.2 78.5 %while.14 = (s32[]{:T(128)}, f32[512,256]{1,0:T(8,128)S(1)}, bf16[3,8,16384]{2,1,0:T(8,128)(2,1)S(1)}, bf16[3,64,16384]{2,1,0:T(8,128)(2,1)}, s32[16384]{0:T(102...) while((s32[]{:T(128)}, f32[512,256]{1,0:T(8,128)S(1)}, bf16[3,8,16384]{2,1,0:T(8,128)(2,1)S(1)}, ...), condition=%wide.region_2.3_spmd.clone, body=%wide.region_0.0_spmd.clone.sunk | while | flops 3227697152 | bytes 13885601 | solution.py:92
  194.2 1.3 dynamic-slice_convert_fusion.4
  195.5 3.1 multiply_reduce_fusion.2
  198.6 0.7 dynamic_slice.41
  199.3 4.7 %fusion.30 = f32[512,256]{1,0:T(8,128)S(1)} fusion(f32[512,2048]{1,0:T(8,128)} %bitcast.31, s32[2048]{0:T(1024)S(1)} %dynamic_slice.41, f32[512,256]{1,0:T(8,128)S(1)} %get-tuple-element.203, pred[]{:T(512)S(6)} %compare.4), kind=kOutput, calls=%fused_computation.4.clone.1 | convolution fusion | flops 3222011904 | bytes 5251073 | tf_op jit(solution)/shard_map/while/body/eval_jaxpr/dot_general | solution.py:90
  204.0 1.3 dynamic-slice_convert_fusion.4
  205.3 3.1 multiply_reduce_fusion.2
  209.1 4.7 %fusion.30 = f32[512,256]{1,0:T(8,128)S(1)} fusion(f32[512,2048]{1,0:T(8,128)} %bitcast.31, s32[2048]{0:T(1024)S(1)} %dynamic_slice.41, f32[512,256]{1,0:T(8,128)S(1)} %get-tuple-element.203, pred[]{:T(512)S(6)} %compare.4), kind=kOutput, calls=%fused_computation.4.clone.1 | convolution fusion | flops 3222011904 | bytes 5251073 | tf_op jit(solution)/shard_map/while/body/eval_jaxpr/dot_general | solution.py:90
  213.8 1.3 dynamic-slice_convert_fusion.4
  215.2 3.1 multiply_reduce_fusion.2
  218.9 4.7 %fusion.30 = f32[512,256]{1,0:T(8,128)S(1)} fusion(f32[512,2048]{1,0:T(8,128)} %bitcast.31, s32[2048]{0:T(1024)S(1)} %dynamic_slice.41, f32[512,256]{1,0:T(8,128)S(1)} %get-tuple-element.203, pred[]{:T(512)S(6)} %compare.4), kind=kOutput, calls=%fused_computation.4.clone.1 | convolution fusion | flops 3222011904 | bytes 5251073 | tf_op jit(solution)/shard_map/while/body/eval_jaxpr/dot_general | solution.py:90
  223.6 1.3 dynamic-slice_convert_fusion.4
  225.0 3.1 multiply_reduce_fusion.2
  228.1 0.7 dynamic_slice.41
  228.8 4.7 %fusion.30 = f32[512,256]{1,0:T(8,128)S(1)} fusion(f32[512,2048]{1,0:T(8,128)} %bitcast.31, s32[2048]{0:T(1024)S(1)} %dynamic_slice.41, f32[512,256]{1,0:T(8,128)S(1)} %get-tuple-element.203, pred[]{:T(512)S(6)} %compare.4), kind=kOutput, calls=%fused_computation.4.clone.1 | convolution fusion | flops 3222011904 | bytes 5251073 | tf_op jit(solution)/shard_map/while/body/eval_jaxpr/dot_general | solution.py:90
  233.5 1.3 dynamic-slice_convert_fusion.4
  234.8 3.1 multiply_reduce_fusion.2
  238.6 4.7 %fusion.30 = f32[512,256]{1,0:T(8,128)S(1)} fusion(f32[512,2048]{1,0:T(8,128)} %bitcast.31, s32[2048]{0:T(1024)S(1)} %dynamic_slice.41, f32[512,256]{1,0:T(8,128)S(1)} %get-tuple-element.203, pred[]{:T(512)S(6)} %compare.4), kind=kOutput, calls=%fused_computation.4.clone.1 | convolution fusion | flops 3222011904 | bytes 5251073 | tf_op jit(solution)/shard_map/while/body/eval_jaxpr/dot_general | solution.py:90
  243.3 1.3 dynamic-slice_convert_fusion.4
  244.6 3.1 multiply_reduce_fusion.2
  248.4 4.7 %fusion.30 = f32[512,256]{1,0:T(8,128)S(1)} fusion(f32[512,2048]{1,0:T(8,128)} %bitcast.31, s32[2048]{0:T(1024)S(1)} %dynamic_slice.41, f32[512,256]{1,0:T(8,128)S(1)} %get-tuple-element.203, pred[]{:T(512)S(6)} %compare.4), kind=kOutput, calls=%fused_computation.4.clone.1 | convolution fusion | flops 3222011904 | bytes 5251073 | tf_op jit(solution)/shard_map/while/body/eval_jaxpr/dot_general | solution.py:90
  253.1 1.3 dynamic-slice_convert_fusion.4
  254.4 3.1 multiply_reduce_fusion.2
  257.5 0.7 dynamic_slice.41
  258.2 4.7 %fusion.30 = f32[512,256]{1,0:T(8,128)S(1)} fusion(f32[512,2048]{1,0:T(8,128)} %bitcast.31, s32[2048]{0:T(1024)S(1)} %dynamic_slice.41, f32[512,256]{1,0:T(8,128)S(1)} %get-tuple-element.203, pred[]{:T(512)S(6)} %compare.4), kind=kOutput, calls=%fused_computation.4.clone.1 | convolution fusion | flops 3222011904 | bytes 5251073 | tf_op jit(solution)/shard_map/while/body/eval_jaxpr/dot_general | solution.py:90
  262.9 1.3 dynamic-slice_convert_fusion.4
  264.3 3.1 multiply_reduce_fusion.2
  267.3 0.7 dynamic_slice.41
  268.0 4.7 %fusion.30 = f32[512,256]{1,0:T(8,128)S(1)} fusion(f32[512,2048]{1,0:T(8,128)} %bitcast.31, s32[2048]{0:T(1024)S(1)} %dynamic_slice.41, f32[512,256]{1,0:T(8,128)S(1)} %get-tuple-element.203, pred[]{:T(512)S(6)} %compare.4), kind=kOutput, calls=%fused_computation.4.clone.1 | convolution fusion | flops 3222011904 | bytes 5251073 | tf_op jit(solution)/shard_map/while/body/eval_jaxpr/dot_general | solution.py:90
  273.0 1.9 fusion.15
  275.4 72.6 %psum.7 = f32[64]{0:T(128)S(1)} all-reduce(f32[64]{0:T(128)S(1)} %dynamic_update_slice.3), channel_id=1, replica_groups=mesh['tile'=32,'mode'=8] {'tile','mode'}, use_global_device_ids=true, to_apply=%region_5.6 | all-reduce | flops 64 | bytes 512 | tf_op jit(solution)/shard_map/psum | solution.py:68
  348.2 7.9 %reduce-scatter.2.cloned.1.call-done = f32[16,512]{1,0:T(8,128)} async-done(((f32[512,512]{1,0:T(8,128)}), f32[16,512]{1,0:T(8,128)}) %reduce-scatter.2.cloned.1.call-update) | async-done | bytes 32784 | tf_op jit(solution)/shard_map/reduce_scatter | solution.py:103
  356.1 0.8 broadcast_multiply_fusion.1
  (42 shorter events, 6.2 us)
Async XLA Ops:
  6.5 26.4 %copy-start = (s32[32,32,8]{1,2,0:T(8,128)S(1)}, s32[32,32,8]{1,2,0:T(8,128)}, u32[]{:S(2)}) copy-start(s32[32,32,8]{1,2,0:T(8,128)} %param.9) | copy-start | bytes 98308
  7.7 7.7 %collective-permute-start = (bf16[8,1,2048]{2,1,0:T(2,128)(2,1)S(1)}, bf16[8,1,2048]{2,1,0:T(2,128)(2,1)S(1)}, u32[]{:S(2)}, u32[]{:S(2)}) collective-permute-start(bf16[8,1,2048]{2,1,0:T(2,128)(2,1)S(1)} %get-tuple-element.160), channel_id=1, source_target_pairs={{0,8},{8,16},{16,24},{24,32},{32,40},{40,48},{48,56},{56,64},{64,7... | collective-permute-start | bytes 98312 | tf_op jit(solution)/shard_map/ppermute | solution.py:20
  9.6 7.6 %collective-permute-start.1 = (bf16[8,1,2048]{2,1,0:T(2,128)(2,1)S(1)}, bf16[8,1,2048]{2,1,0:T(2,128)(2,1)S(1)}, u32[]{:S(2)}, u32[]{:S(2)}) collective-permute-start(bf16[8,1,2048]{2,1,0:T(2,128)(2,1)S(1)} %get-tuple-element.161), channel_id=1, source_target_pairs={{8,0},{16,8},{24,16},{32,24},{40,32},{48,40},{56,48},{64,56},{72,6... | collective-permute-start | bytes 98312 | tf_op jit(solution)/shard_map/ppermute | solution.py:22
  23.4 8.8 %copy-start.4 = (s32[8,2048]{1,0:T(8,128)S(1)}, s32[8,2048]{1,0:T(8,128)}, u32[]{:S(2)}) copy-start(s32[8,2048]{1,0:T(8,128)} %param.8) | copy-start | bytes 196612
  23.4 9.6 %copy-start.3 = (f32[8,2048]{1,0:T(8,128)S(1)}, f32[8,2048]{1,0:T(8,128)}, u32[]{:S(2)}) copy-start(f32[8,2048]{1,0:T(8,128)} %param.7) | copy-start | bytes 196612
  23.4 149.9 %all-to-all-start = ((bf16[8,3,8,8,2048]{4,2,3,1,0:T(8,128)(2,1)}), bf16[8,3,8,8,2048]{4,2,3,1,0:T(8,128)(2,1)}, u32[]{:S(2)}, u32[]{:S(2)}) async-start(bf16[8,3,8,8,2048]{4,2,3,1,0:T(8,128)(2,1)} %stack.49), calls=%async_computation | async-start | bytes 12582912 | tf_op jit(solution)/shard_map/all_to_all | solution.py:70
  32.0 324.1 %reduce-scatter.2.cloned.1.call-start = ((), (), s32[]{:S(2)}) async-start(), calls=%async_computation.2 | async-start | bytes 1081344 | tf_op jit(solution)/shard_map/reduce_scatter | solution.py:103
  272.7 2.2 copy-start.1
  272.7 2.2 copy-start.2
Sparse Core Ops, SparseCore 0:
  275.0 81.0 reduce-scatter.1
